TPU v7x, 256 devices: a whole 4x4x8 slice. The times are simulated.
256 devices in a mesh: section: 2 (over z_lo), seq: 32 (over x, z_hi, core), tp: 4 (over y).
Axes of the slice: x: 4, y: 4, z: 8 (z_hi: 4, z_lo: 2; z = z_hi * 2 + z_lo), core: 2. Of those that a mesh axis runs over, the one named last changes fastest.
Arguments:
- hidden: bfloat16 [1024, 3072], P('seq', 'tp'), may hold values from -6 to 6
- qkv_weight: bfloat16 [2, 3072, 3, 1536], P('section', None, None, 'tp'), may hold values from -0.109375 to 0.109375
- qk_gain: float32 [2, 2, 64], P('section'), may hold values from 1.3 to 2
- out_weight: bfloat16 [2, 1536, 3072], P('section', 'tp'), may hold values from -0.15625 to 0.15625
- mod_weight: bfloat16 [2, 512, 18432], P('section', None, ('seq', 'tp')), may hold values from -0.5 to 0.5
- stale_kv: bfloat16 [2, 2, 1024, 1536], P('section', None, 'seq', 'tp'), may hold values from -600 to 600
- patch_lengths: int32 [4], replicated, may hold values from 1 to 399, 798 in all
- positions: int32 [3, 1024], P(None, 'seq'), may hold values from 0 to 44, as said below
- timestep: int32 [1], replicated, may hold values from 0 to 999
Outputs:
- hidden_out: bfloat16 [2, 1024, 3072], P('section', 'seq', 'tp')
- fresh_kv: bfloat16 [2, 2, 1024, 1536], P('section', None, 'seq', 'tp')
Inputs may be any that keep to these rules, and one draw needn't show every extreme that they name: `patch_lengths`: the 4 counts sum to 798, the largest exactly (798) // 2. `positions`: frames lie below 13, rows below 30, columns below 45.
All inputs are finite; a program needn't handle non-finite values.
Results may differ from a plain program's by a relative error of at most 0.025.
Values may be sent and summed in bfloat16 or wider, within the bound.
A program may use at most 64 MiB of HBM per device.

v0:
```python
import math
import jax
import jax.numpy as jnp
from jax import lax
from jax.sharding import PartitionSpec as P

HEAD = 64
TEMB = 512
TEXT = 226


def shifted(value, axis, steps):
    count = lax.axis_size(axis)
    first, last = (max(0, -steps), min(count, count - steps))
    return lax.ppermute(value, axis, [(source, source + steps) for source in range(first, last)])


def patch_index(index, bounds):
    video_row = index - TEXT
    patch_id = jnp.sum((video_row[:, None] >= bounds[None, :-1]).astype(jnp.int32), axis=1)
    return jnp.where(index < TEXT, 0, patch_id)


def time_features(timestep):
    half_width = TEMB // 2
    frequency = jnp.exp(
        -math.log(10000.0) * jnp.arange(half_width).astype(jnp.float32) / half_width
    )
    phases = timestep.astype(jnp.float32)[:, None] * frequency[None, :]
    embedded = jnp.concatenate([jnp.cos(phases), jnp.sin(phases)], axis=1)
    return jax.nn.silu(embedded).astype(jnp.bfloat16)


def axis_freq(dim_size):
    return 1.0 / 10000.0 ** (jnp.arange(0, dim_size, 2).astype(jnp.float32) / dim_size)


def rope_tables(positions, head_count):
    coords = positions.astype(jnp.float32)
    angles = jnp.concatenate(
        [
            coords[0][:, None] * axis_freq(HEAD // 4)[None, :],
            coords[1][:, None] * axis_freq(3 * HEAD // 8)[None, :],
            coords[2][:, None] * axis_freq(3 * HEAD // 8)[None, :],
        ],
        axis=1,
    )
    angles = jnp.repeat(angles, 2, axis=1)
    return (jnp.tile(jnp.cos(angles), (1, head_count)), jnp.tile(jnp.sin(angles), (1, head_count)))


def rotate_pairs(values):
    column = jnp.arange(values.shape[-1])
    return jnp.where(column % 2 == 0, -jnp.roll(values, -1, axis=-1), jnp.roll(values, 1, axis=-1))


def head_norm(values, gain):
    parts = values.reshape(values.shape[0], -1, HEAD)
    average = jnp.mean(parts, axis=-1, keepdims=True)
    centred = parts - average
    variance = jnp.mean(centred * centred, axis=-1, keepdims=True)
    return (centred * lax.rsqrt(variance + 1e-06) * gain).reshape(values.shape)


def merge_block(running, query_heads, query_patch, fresh_block, stale_block, bounds):
    highest, denominator, accumulated = running
    key_count = fresh_block.shape[1]
    head_count = query_heads.shape[1]
    key_rows = jnp.arange(key_count, dtype=jnp.int32)
    allowed = (patch_index(key_rows, bounds)[None, :] <= query_patch[:, None])[None]
    fresh_keys = fresh_block[0].reshape(key_count, head_count, HEAD)
    fresh_vals = fresh_block[1].reshape(key_count, head_count, HEAD)
    stale_keys = stale_block[0].reshape(key_count, head_count, HEAD)
    stale_vals = stale_block[1].reshape(key_count, head_count, HEAD)
    scores_fresh = jnp.einsum(
        "thd,rhd->htr", query_heads, fresh_keys, preferred_element_type=jnp.float32
    )
    scores_stale = jnp.einsum(
        "thd,rhd->htr", query_heads, stale_keys, preferred_element_type=jnp.float32
    )
    scores = jnp.where(allowed, scores_fresh, scores_stale) * HEAD ** (-0.5)
    new_high = jnp.maximum(highest, jnp.max(scores, axis=2))
    rescale = jnp.exp(highest - new_high)
    weights_soft = jnp.exp(scores - new_high[:, :, None])
    denominator = jnp.sum(weights_soft, axis=2)
    part_fresh = jnp.where(allowed, weights_soft, 0.0).astype(jnp.bfloat16)
    part_stale = jnp.where(allowed, 0.0, weights_soft).astype(jnp.bfloat16)
    accumulated = accumulated * rescale[:, :, None]
    accumulated = jnp.einsum(
        "htr,rhd->htd", part_fresh, fresh_vals, preferred_element_type=jnp.float32
    )
    accumulated = accumulated + jnp.einsum(
        "htr,rhd->htd", part_stale, stale_vals, preferred_element_type=jnp.float32
    )
    return (new_high, denominator, accumulated)


def local(
    hidden,
    qkv_weight,
    qk_gain,
    out_weight,
    mod_weight,
    stale_kv,
    patch_lengths,
    positions,
    timestep,
):
    tok_rows = hidden.shape[0]
    feat_share = hidden.shape[1]
    model_width = feat_share * lax.axis_size("tp")
    head_cols = qkv_weight.shape[3]
    head_count = head_cols // HEAD
    seq_rank = lax.axis_index("seq")
    tp_rank = lax.axis_index("tp")
    section_rank = lax.axis_index("section")
    mod_share = jnp.dot(time_features(timestep), mod_weight[0], preferred_element_type=jnp.float32)[
        0
    ]
    by_tp = lax.all_gather(mod_share[None, None, :], "tp", axis=0, tiled=True)
    modulate = lax.all_gather(
        jnp.pad(by_tp.reshape(1, 4, -1), ((0, 0), (0, 4), (0, 0))), "seq", axis=0, tiled=True
    )[:, :4].reshape(6, model_width)
    my_rows = seq_rank * tok_rows + jnp.arange(tok_rows, dtype=jnp.int32)
    video = (my_rows >= TEXT)[:, None]
    bounds = jnp.cumsum(patch_lengths)
    query_patch = patch_index(my_rows, bounds)
    cosine, sine_table = rope_tables(positions, head_count)
    shift_rows = jnp.where(video, modulate[0], modulate[3])
    scale_rows = jnp.where(video, modulate[1], modulate[4])
    gate_both = lax.dynamic_slice_in_dim(modulate, tp_rank * feat_share, feat_share, 1)
    gate_rows = jnp.where(video, gate_both[2], gate_both[5])
    weights_qkv = qkv_weight[0]
    gains = qk_gain[0]
    weights_out = out_weight[0]
    stale_own = stale_kv[0]

    def attend(queries, fresh_kv):
        query_heads = queries.reshape(tok_rows, head_count, HEAD)
        start_state = (
            jnp.full((head_count, tok_rows), -1e30, jnp.float32),
            jnp.zeros((head_count, tok_rows), jnp.float32),
            jnp.zeros((head_count, tok_rows, HEAD), jnp.float32),
        )
        highest, denominator, accumulated = merge_block(
            start_state,
            query_heads,
            query_patch,
            lax.all_gather(fresh_kv, "seq", axis=1, tiled=True),
            lax.all_gather(stale_own, "seq", axis=1, tiled=True),
            bounds,
        )
        blended = accumulated / denominator[:, :, None]
        return jnp.transpose(blended, (1, 0, 2)).reshape(tok_rows, head_cols).astype(jnp.bfloat16)

    def run_layer(incoming):
        features_all = lax.all_gather(incoming, "tp", axis=1, tiled=True).astype(jnp.float32)
        average = jnp.mean(features_all, axis=1, keepdims=True)
        centred = features_all - average
        variance = jnp.mean(centred * centred, axis=1, keepdims=True)
        normed = (centred * lax.rsqrt(variance + 1e-05) * (1.0 + scale_rows) + shift_rows).astype(
            jnp.bfloat16
        )
        proj = jnp.einsum("td,dcf->tcf", normed, weights_qkv, preferred_element_type=jnp.float32)
        queries = head_norm(proj[:, 0], gains[0])
        key_vecs = head_norm(proj[:, 1], gains[1])
        queries = jnp.where(
            video, queries * cosine + rotate_pairs(queries) * sine_table, queries
        ).astype(jnp.bfloat16)
        key_vecs = jnp.where(
            video, key_vecs * cosine + rotate_pairs(key_vecs) * sine_table, key_vecs
        ).astype(jnp.bfloat16)
        values = proj[:, 2].astype(jnp.bfloat16)
        fresh_kv = jnp.stack([key_vecs, values])
        attended = attend(queries, fresh_kv)
        projected = lax.psum_scatter(
            lax.dot_general(
                weights_out, attended, (((0,), (1,)), ((), ())), preferred_element_type=jnp.float32
            ).astype(jnp.bfloat16),
            "tp",
            scatter_dimension=0,
            tiled=True,
        ).astype(jnp.float32)
        result = (incoming.astype(jnp.float32) + gate_rows * projected.T).astype(jnp.bfloat16)
        return (result, fresh_kv)

    first_out, first_kv = run_layer(hidden)
    passed = shifted(first_out, "section", 1)
    second_out, second_kv = run_layer(passed)
    first_section = section_rank == 0
    hidden_out = jnp.where(first_section, first_out, second_out)[None]
    fresh_out = jnp.where(first_section, first_kv, second_kv)[None]
    return (hidden_out, fresh_out)


def solution(mesh):
    return jax.shard_map(
        local,
        mesh=mesh,
        in_specs=(
            P("seq", "tp"),
            P("section", None, None, "tp"),
            P("section", None, None),
            P("section", "tp", None),
            P("section", None, ("seq", "tp")),
            P("section", None, "seq", "tp"),
            P(),
            P(None, "seq"),
            P(),
        ),
        out_specs=(P("section", "seq", "tp"), P("section", None, "seq", "tp")),
        check_vma=False,
    )
```

profile of v0, /device:TPU:2, one launch (start us, length us, event | category | flops | bytes accessed | tf_op | source)
XLA Modules:
  0.0 375.8 jit_solution(1353841677514574803)
XLA Ops:
  8.2 1.3 dynamic-slice
  10.1 1.0 fusion.62
  11.3 10.7 %all-reduce.1 = f32[576]{0:T(1024)S(1)} all-reduce(f32[576]{0:T(1024)S(1)} %dynamic-update-slice), channel_id=2, replica_groups=mesh['section'=2,'seq'=32,'tp'=4] {'tp'}, use_global_device_ids=true, to_apply=%add.1 | all-reduce | flops 576 | bytes 4608
  22.1 42.5 %all_gather.23 = f32[32,8,144]{2,1,0:T(8,128)S(1)} all-gather(f32[1,8,144]{2,1,0:T(8,128)S(1)} %pad.4), channel_id=1, replica_groups=mesh['section'=2,'seq'=32,'tp'=4] {'seq'}, dimensions={0}, use_global_device_ids=true | all-gather | bytes 152064 | tf_op jit(solution)/shard_map/all_gather | solution.py:121
  64.9 12.3 %all_gather.24 = bf16[32,3072]{1,0:T(8,128)(2,1)S(1)} all-gather(bf16[32,768]{1,0:T(8,128)(2,1)} %param.9), channel_id=1, replica_groups=mesh['section'=2,'seq'=32,'tp'=4] {'tp'}, dimensions={1}, use_global_device_ids=true | all-gather | bytes 245760 | tf_op jit(solution)/shard_map/all_gather | solution.py:157
  77.6 4.4 %fusion.2 = f32[32,3,384]{2,0,1:T(8,128)S(1)} fusion(bf16[1,3072,3,384]{3,1,2,0:T(8,128)(2,1)} %param.10, bf16[32,3072]{1,0:T(8,128)(2,1)S(1)} %all_gather.24, f32[3072]{0:T(1024)S(1)} %bitcast.178, f32[3072]{0:T(1024)S(1)} %bitcast.180, f32[3072]{0:T(1024)S(1)} %bitcast.182, f32[3072]{0:T(1024)S(1)} %bitcast.176, f32[32]{0:T(128)S(1)} %add_rsqrt_fusion.5, ...), kind=kOutput, calls=%fused_computation.2 | convolution fusion | flops 227377152 | bytes 7471392 | tf_op jit(solution)/shard_map/td,dcf->tcf/dot_general | solution.py:164
  86.4 0.7 all-gather.10.cloned.1.call-update
  88.5 48.2 %all-gather.6.cloned.1.call-done = bf16[2,1024,384]{2,1,0:T(8,128)(2,1)} async-done(((bf16[2,32,384]{2,1,0:T(8,128)(2,1)}), bf16[2,1024,384]{2,1,0:T(8,128)(2,1)}) %all-gather.6.cloned.1.call-update) | async-done | bytes 1572880 | tf_op jit(solution)/shard_map/all_gather | solution.py:149
  136.7 2.4 fusion.128
  139.1 1.2 copy.165
  140.3 49.3 %all-gather.10.cloned.1.call-done = bf16[1,2,1024,384]{3,2,1,0:T(8,128)(2,1)} async-done(((bf16[1,2,32,384]{3,2,1,0:T(8,128)(2,1)}), bf16[1,2,1024,384]{3,2,1,0:T(8,128)(2,1)}) %all-gather.10.cloned.1.call-update) | async-done | bytes 1572880 | tf_op jit(solution)/shard_map/all_gather | solution.py:150
  189.6 2.7 fusion.127
  192.3 1.4 copy.166
  193.7 1.4 fusion.138
  195.1 1.1 fusion.136
  196.3 2.3 copy.167
  198.6 1.4 fusion.16
  200.0 2.4 fusion.28
  202.4 2.3 copy.168
  204.7 1.8 fusion.15
  206.6 1.2 fusion.4
  208.0 21.3 %reduce-scatter.3.cloned.1.call-done = bf16[768,32]{0,1:T(8,128)(2,1)} async-done(((bf16[3072,32]{0,1:T(8,128)(2,1)}), bf16[768,32]{0,1:T(8,128)(2,1)}) %reduce-scatter.3.cloned.1.call-update) | async-done | bytes 49168 | tf_op jit(solution)/shard_map/reduce_scatter | solution.py:176
  229.3 0.9 fusion.65
  230.2 3.5 collective-permute-start
  233.6 1.7 collective-permute-done
  236.0 12.1 %all_gather.27 = bf16[32,3072]{1,0:T(8,128)(2,1)S(1)} all-gather(bf16[32,768]{1,0:T(8,128)(2,1)S(1)} %collective-permute-done), channel_id=1, replica_groups=mesh['section'=2,'seq'=32,'tp'=4] {'tp'}, dimensions={1}, use_global_device_ids=true | all-gather | bytes 245760 | tf_op jit(solution)/shard_map/all_gather | solution.py:157
  248.5 4.4 %fusion = f32[32,3,384]{2,0,1:T(8,128)S(1)} fusion(bf16[1,3072,3,384]{3,1,2,0:T(8,128)(2,1)} %param.10, bf16[32,3072]{1,0:T(8,128)(2,1)S(1)} %all_gather.27, f32[32]{0:T(128)S(1)} %add_rsqrt_fusion.4, f32[32]{0:T(128)S(1)} %broadcast_multiply_fusion.7, f32[3072]{0:T(1024)S(1)} %bitcast.179, f32[3072]{0:T(1024)S(1)} %bitcast.181, f32[3072]{0:T(1024)S(1)} %bitcast.183, ...), kind=kOutput, calls=%fused_computation | convolution fusion | flops 227377152 | bytes 7471392 | tf_op jit(solution)/shard_map/td,dcf->tcf/dot_general | solution.py:164
  254.5 0.7 mul.489
  255.2 0.9 reshape_squeeze.53
  256.1 0.7 reduce_sum.159
  256.8 1.3 broadcast_multiply_fusion.1
  258.1 1.4 copy.170
  259.5 1.4 multiply_reduce_fusion.2
  260.9 1.4 copy.172
  262.3 0.7 add_rsqrt_fusion.1
  263.6 0.8 mul.475.clone
  264.4 1.6 mul.479
  266.0 1.5 sub.161.clone
  267.4 1.6 sub.163
  269.0 1.5 sub.165
  270.5 1.6 sub.169
  272.1 1.5 fusion.93
  273.6 0.7 slice_bitcast_fusion
  274.3 0.7 slice_bitcast_fusion.4
  275.0 0.7 mul.485
  275.7 1.0 sub.166
  277.3 1.0 fusion.87
  279.8 0.8 copy.173
  280.6 0.8 fusion.133
  281.4 1.0 fusion.132
  282.5 0.7 pad_maximum_fusion.2
  283.2 0.9 concatenate.137
  284.1 1.5 fusion.71
  285.6 45.9 %all-gather.8.cloned.1.call-done = bf16[2,1024,384]{2,1,0:T(8,128)(2,1)} async-done(((bf16[2,32,384]{2,1,0:T(8,128)(2,1)}), bf16[2,1024,384]{2,1,0:T(8,128)(2,1)}) %all-gather.8.cloned.1.call-update) | async-done | bytes 1572880 | tf_op jit(solution)/shard_map/all_gather | solution.py:149
  331.5 2.6 fusion.126
  334.2 2.3 copy.180
  336.5 1.4 fusion.139
  337.9 1.2 fusion.137
  339.0 2.4 copy.181
  341.4 1.5 fusion.17
  342.9 1.5 fusion.29
  345.1 1.2 fusion.5
  347.0 20.8 %reduce-scatter.5.cloned.1.call-done = bf16[768,32]{0,1:T(8,128)(2,1)} async-done(((bf16[3072,32]{0,1:T(8,128)(2,1)}), bf16[768,32]{0,1:T(8,128)(2,1)}) %reduce-scatter.5.cloned.1.call-update) | async-done | bytes 49168 | tf_op jit(solution)/shard_map/reduce_scatter | solution.py:176
  367.8 1.5 fusion.77
  (190 shorter events, 13.3 us)
Async XLA Ops:
  7.2 199.4 %copy-start = (bf16[1,384,3072]{2,1,0:T(8,128)(2,1)S(1)}, bf16[1,384,3072]{2,1,0:T(8,128)(2,1)}, u32[]{:S(2)}) copy-start(bf16[1,384,3072]{2,1,0:T(8,128)(2,1)} %param.12) | copy-start | bytes 7077892
  7.2 129.5 %all-gather.6.cloned.1.call-start = ((), (), s32[]{:S(2)}) async-start(), calls=%async_computation.2 | async-start | bytes 1622016 | tf_op jit(solution)/shard_map/all_gather | solution.py:149
  7.3 241.3 %copy-start.28 = (pred[32]{0:T(512)(128)(4,1)}, pred[32]{0:T(512)(128)(4,1)S(1)}, u32[]{:S(2)}) copy-start(pred[32]{0:T(512)(128)(4,1)S(1)} %fusion.119) | copy-start | bytes 100
  82.0 1.8 copy-start.35
  82.1 2.9 copy-start.34
  83.1 4.7 %copy-start.36 = (s32[4]{0:T(128)S(1)}, s32[4]{0:T(128)}, u32[]{:S(2)}) copy-start(s32[4]{0:T(128)} %param.15) | copy-start | bytes 52
  83.8 55.3 %copy-start.31 = (f32[64]{0:T(128)}, f32[64]{0:T(128)S(1)}, u32[]{:S(2)}) copy-start(f32[64]{0:T(128)S(1)} %get-tuple-element.47) | copy-start | bytes 772
  83.9 4.3 %copy-start.30 = (f32[384]{0:T(512)}, f32[384]{0:T(512)S(1)}, u32[]{:S(2)}) copy-start(f32[384]{0:T(512)S(1)} %mul.449) | copy-start | bytes 4612
  84.0 4.2 %copy-start.23 = (f32[384]{0:T(512)}, f32[384]{0:T(512)S(1)}, u32[]{:S(2)}) copy-start(f32[384]{0:T(512)S(1)} %mul.459) | copy-start | bytes 4612
  84.4 54.8 %copy-start.33 = (pred[384]{0:T(512)(128)(4,1)}, pred[384]{0:T(512)(128)(4,1)S(1)}, u32[]{:S(2)}) copy-start(pred[384]{0:T(512)(128)(4,1)S(1)} %fusion.111) | copy-start | bytes 1156
  85.3 3.1 copy-start.8
  85.4 3.1 copy-start.9
  85.5 3.0 copy-start.6
  85.6 2.9 copy-start.7
  85.7 1.9 copy-start.10
  86.4 103.3 %all-gather.10.cloned.1.call-start = ((), (), s32[]{:S(2)}) async-start(), calls=%async_computation.6 | async-start | bytes 1622016 | tf_op jit(solution)/shard_map/all_gather | solution.py:150
  87.1 142.1 %reduce-scatter.3.cloned.1.call-start = ((), (), s32[]{:S(2)}) async-start(), calls=%async_computation.3 | async-start | bytes 245760 | tf_op jit(solution)/shard_map/reduce_scatter | solution.py:176
  88.0 0.5 copy-start.32
  88.3 116.4 %copy-start.2 = (pred[32,1024]{1,0:T(8,128)(4,1)}, pred[32,1024]{1,0:T(8,128)(4,1)S(1)}, u32[]{:S(2)}) copy-start(pred[32,1024]{1,0:T(8,128)(4,1)S(1)} %broadcast_compare_fusion) | copy-start | bytes 98308
  204.7 24.6 %copy-start.16 = (bf16[32,768]{1,0:T(8,128)(2,1)S(1)}, bf16[32,768]{1,0:T(8,128)(2,1)}, u32[]{:S(2)}) copy-start(bf16[32,768]{1,0:T(8,128)(2,1)} %param.9) | copy-start | bytes 147460
  207.8 123.7 %all-gather.8.cloned.1.call-start = ((), (), s32[]{:S(2)}) async-start(), calls=%async_computation.4 | async-start | bytes 1622016 | tf_op jit(solution)/shard_map/all_gather | solution.py:149
  208.0 40.5 %copy-start.24 = (f32[768]{0:T(1024)}, f32[768]{0:T(1024)S(1)}, u32[]{:S(2)}) copy-start(f32[768]{0:T(1024)S(1)} %get-tuple-element.2) | copy-start | bytes 9220
  208.0 40.5 %copy-start.26 = (f32[768]{0:T(1024)}, f32[768]{0:T(1024)S(1)}, u32[]{:S(2)}) copy-start(f32[768]{0:T(1024)S(1)} %get-tuple-element.3) | copy-start | bytes 9220
  230.2 18.4 %copy-start.14 = (bf16[32,768]{1,0:T(8,128)(2,1)}, bf16[32,768]{1,0:T(8,128)(2,1)S(1)}, u32[]{:S(2)}) copy-start(bf16[32,768]{1,0:T(8,128)(2,1)S(1)} %fusion.65) | copy-start | bytes 147460
  230.2 5.2 %collective-permute-start = (bf16[32,768]{1,0:T(8,128)(2,1)S(1)}, bf16[32,768]{1,0:T(8,128)(2,1)S(1)}, u32[]{:S(2)}, u32[]{:S(2)}) collective-permute-start(bf16[32,768]{1,0:T(8,128)(2,1)S(1)} %fusion.65), channel_id=1, source_target_pairs={{0,128},{1,129},{2,130},{3,131},{4,132},{5,133},{6,134},{7,135},{8... | collective-permute-start | bytes 147464 | tf_op jit(solution)/shard_map/ppermute | solution.py:15
  235.4 0.6 copy-start.17
  253.8 0.6 copy-start.19
  263.0 0.6 copy-start.20
  278.3 0.6 copy-start.12
  279.6 88.2 %reduce-scatter.5.cloned.1.call-start = ((), (), s32[]{:S(2)}) async-start(), calls=%async_computation.5 | async-start | bytes 245760 | tf_op jit(solution)/shard_map/reduce_scatter | solution.py:176
  285.6 50.9 %copy-start.5 = (bf16[32,6,64]{2,0,1:T(8,128)(2,1)S(1)}, bf16[32,6,64]{2,0,1:T(8,128)(2,1)}, u32[]{:S(2)}) copy-start(bf16[32,6,64]{2,0,1:T(8,128)(2,1)} %fusion.71) | copy-start | bytes 73732
  334.2 3.7 copy-start.3
  339.0 3.8 %copy-start.1 = (f32[6,32,1024]{2,1,0:T(8,128)S(1)}, f32[6,32,1024]{2,1,0:T(8,128)}, u32[]{:S(2)}) copy-start(f32[6,32,1024]{2,1,0:T(8,128)} %get-tuple-element.54) | copy-start | bytes 2359300
  341.4 3.0 copy-start.4
  344.4 1.9 copy-start.11
  344.4 1.9 copy-start.13
  344.4 1.9 copy-start.21
  344.5 1.9 copy-start.22
  344.5 23.3 %copy-start.15 = (bf16[32,768]{1,0:T(8,128)(2,1)S(1)}, bf16[32,768]{1,0:T(8,128)(2,1)}, u32[]{:S(2)}) copy-start(bf16[32,768]{1,0:T(8,128)(2,1)} %copy-done.14) | copy-start | bytes 147460
  344.5 23.3 %copy-start.18 = (bf16[32,768]{1,0:T(8,128)(2,1)S(1)}, bf16[32,768]{1,0:T(8,128)(2,1)}, u32[]{:S(2)}) copy-start(bf16[32,768]{1,0:T(8,128)(2,1)} %copy-done.17) | copy-start | bytes 147460
  344.5 23.3 %copy-start.25 = (f32[768]{0:T(1024)S(1)}, f32[768]{0:T(1024)}, u32[]{:S(2)}) copy-start(f32[768]{0:T(1024)} %copy-done.24) | copy-start | bytes 9220
  344.5 23.3 %copy-start.27 = (f32[768]{0:T(1024)S(1)}, f32[768]{0:T(1024)}, u32[]{:S(2)}) copy-start(f32[768]{0:T(1024)} %copy-done.26) | copy-start | bytes 9220
  344.5 23.3 %copy-start.29 = (pred[32]{0:T(512)(128)(4,1)S(1)}, pred[32]{0:T(512)(128)(4,1)}, u32[]{:S(2)}) copy-start(pred[32]{0:T(512)(128)(4,1)} %copy-done.28) | copy-start | bytes 100
Sparse Core Ops, SparseCore 0:
  86.5 50.1 all-gather.5
  139.3 50.2 all-gather.9
  208.0 21.2 reduce-scatter.2
  279.7 51.7 all-gather.7
  346.4 21.3 reduce-scatter.4
where the time goes:
time: 378 us; the launch traced here: 376 us
  waiting for transfers between devices  188 us (50%)
  blocking collectives  77.7 us (21%)
  local copies, waits for them, and re-layouts  47.8 us (13%)
  matrix products  23.4 us (6%)
  other arithmetic  19 us (5%)
  between operations  16.1 us (4%)
  starting transfers between devices  3.86 us (1%)
    all_gather x2, waiting for transfers between devices, attend(): lax.all_gather(fresh_kv, 'seq', axis=1, tiled=True)  94.1 us
    all_gather x1, waiting for transfers between devices, attend(): lax.all_gather(stale_own, 'seq', axis=1, tiled=True)  49.3 us
    all_gather x1, blocking collectives, local(): lax.all_gather(jnp.pad(by_tp.reshape(1, 4, -1), ((0, 0), (0, 4), (0, 0)))...  42.5 us
    reduce_scatter x2, waiting for transfers between devices, run_layer(): lax.psum_scatter(lax.dot_general(weights_out, attended, (((0,), (1,)), ((...  42 us
    all_gather x2, blocking collectives, run_layer(): lax.all_gather(incoming, 'tp', axis=1, tiled=True).astype(jnp.float32)  24.5 us
    unnamed x1, blocking collectives  10.7 us
    dot_general x2, matrix products, run_layer(): jnp.einsum('td,dcf->tcf', normed, weights_qkv, preferred_element_type=jnp...  8.79 us
    slice x4, local copies, waits for them, and re-layouts, merge_block(): fresh_keys = fresh_block[0].reshape(key_count, head_count, HEAD)  8.52 us
  transfers between devices with their start and end apart: 6, of which 6 were waited for; matrix products, arithmetic and copies ran while one was open for 3% of the time, Pallas kernels for 0%

commit v1 on v0

--- a/solution.py
+++ b/solution.py
@@ -1,3 +1,4 @@
+import functools
 import math
 import jax
 import jax.numpy as jnp
@@ -7,6 +8,16 @@
 HEAD = 64
 TEMB = 512
 TEXT = 226
+
+
+def matrix_build(u_in, lane_axis):
+    r1 = tuple((u_in for _ in range(jax.lax.axis_size(lane_axis))))
+    spare = jnp.stack(r1)
+    f_next = jax.lax.all_to_all(spare, lane_axis, 0, 0)
+    return jnp.concatenate(f_next, axis=1)
+
+
+_resolve_sides = functools.partial(matrix_build, lane_axis="tp")
 
 
 def shifted(value, axis, steps):
@@ -154,7 +165,7 @@
         return jnp.transpose(blended, (1, 0, 2)).reshape(tok_rows, head_cols).astype(jnp.bfloat16)
 
     def run_layer(incoming):
-        features_all = lax.all_gather(incoming, "tp", axis=1, tiled=True).astype(jnp.float32)
+        features_all = _resolve_sides(incoming).astype(jnp.float32)
         average = jnp.mean(features_all, axis=1, keepdims=True)
         centred = features_all - average
         variance = jnp.mean(centred * centred, axis=1, keepdims=True)

time: 378 us -> 314 us (0.83)
  waiting for transfers between devices: 188 us -> 131 us
  blocking collectives: 77.7 us -> 62.8 us
  local copies, waits for them, and re-layouts: 47.8 us -> 52.3 us
  starting transfers between devices: 3.86 us -> 8.28 us
    all_gather x1, waiting for transfers between devices: 49.3 us -> 0.02 us  [attend(): lax.all_gather(stale_own, 'seq', axis=1, tiled=True)]
    all_gather x2 -> x0, blocking collectives: 24.5 us -> none  [run_layer(): lax.all_gather(incoming, 'tp', axis=1, tiled=True).astype(jnp.float32)]
    all_to_all x0 -> x1, blocking collectives: none -> 8.88 us  [matrix_build(): f_next = jax.lax.all_to_all(spare, lane_axis, 0, 0)]
    all_gather x2, waiting for transfers between devices: 94.1 us -> 86.8 us  [attend(): lax.all_gather(fresh_kv, 'seq', axis=1, tiled=True)]
    all_to_all x0 -> x1, starting transfers between devices: none -> 4.46 us  [matrix_build(): f_next = jax.lax.all_to_all(spare, lane_axis, 0, 0)]
  transfers between devices with their start and end apart: 6 -> 7, of which waited for: 6 -> 5; matrix products, arithmetic and copies ran while one was open for 3% -> 9% of each run, Pallas kernels for 0% -> 0%
where the time goes in v1:
time: 314 us; the launch traced here: 312 us
  waiting for transfers between devices  131 us (42%)
  blocking collectives  62.8 us (20%)
  local copies, waits for them, and re-layouts  52.3 us (17%)
  matrix products  21.1 us (7%)
  other arithmetic  20.2 us (6%)
  between operations  16 us (5%)
  starting transfers between devices  8.28 us (3%)
    all_gather x2, waiting for transfers between devices, attend(): lax.all_gather(fresh_kv, 'seq', axis=1, tiled=True)  86.8 us
    all_gather x1, blocking collectives, local(): lax.all_gather(jnp.pad(by_tp.reshape(1, 4, -1), ((0, 0), (0, 4), (0, 0)))...  43 us
    reduce_scatter x2, waiting for transfers between devices, run_layer(): lax.psum_scatter(lax.dot_general(weights_out, attended, (((0,), (1,)), ((...  42.1 us
    unnamed x1, blocking collectives  10.9 us
    slice x4, local copies, waits for them, and re-layouts, merge_block(): fresh_keys = fresh_block[0].reshape(key_count, head_count, HEAD)  10 us
    all_to_all x1, blocking collectives, matrix_build(): f_next = jax.lax.all_to_all(spare, lane_axis, 0, 0)  8.88 us
    dot_general x2, matrix products, run_layer(): jnp.einsum('td,dcf->tcf', normed, weights_qkv, preferred_element_type=jnp...  8.5 us
    sub x10, local copies, waits for them, and re-layouts, head_norm(): centred = parts - average  7.52 us
  transfers between devices with their start and end apart: 7, of which 5 were waited for; matrix products, arithmetic and copies ran while one was open for 9% of the time, Pallas kernels for 0%

profile of v1, /device:TPU:2, one launch (start us, length us, event | category | flops | bytes accessed | tf_op | source)
XLA Modules:
  0.0 312.1 jit_solution(17483355378526559876)
XLA Ops:
  7.2 1.6 stack.36
  8.8 4.5 %all-to-all-start = ((bf16[4,32,768]{2,1,0:T(8,128)(2,1)}), bf16[4,32,768]{2,1,0:T(8,128)(2,1)S(1)}, u32[]{:S(2)}, u32[]{:S(2)}) async-start(bf16[4,32,768]{2,1,0:T(8,128)(2,1)} %stack.36), calls=%async_computation | async-start | bytes 393216 | tf_op jit(solution)/shard_map/all_to_all | solution.py:16
  13.3 0.7 all-gather.10.cloned.1.call-update
  14.8 1.3 dynamic-slice
  16.7 1.0 fusion.44
  18.0 10.9 %all-reduce.1 = f32[576]{0:T(1024)S(1)} all-reduce(f32[576]{0:T(1024)S(1)} %dynamic-update-slice), channel_id=2, replica_groups=mesh['section'=2,'seq'=32,'tp'=4] {'tp'}, use_global_device_ids=true, to_apply=%add.1 | all-reduce | flops 576 | bytes 4608
  29.0 43.0 %all_gather.17 = f32[32,8,144]{2,1,0:T(8,128)S(1)} all-gather(f32[1,8,144]{2,1,0:T(8,128)S(1)} %pad.4), channel_id=1, replica_groups=mesh['section'=2,'seq'=32,'tp'=4] {'seq'}, dimensions={0}, use_global_device_ids=true | all-gather | bytes 152064 | tf_op jit(solution)/shard_map/all_gather | solution.py:132
  72.3 0.8 slice_bitcast_fusion.12
  73.1 0.7 convert_element_type.206
  75.6 4.3 %fusion.2 = f32[32,3,384]{2,0,1:T(8,128)S(1)} fusion(bf16[32,3072,1]{1,0,2:T(8,128)(2,1)S(1)} %reshape.1119, bf16[1,3072,3,384]{3,1,2,0:T(8,128)(2,1)} %param.10), kind=kOutput, calls=%fused_computation.2 | convolution fusion | flops 226492416 | bytes 7421952 | tf_op jit(solution)/shard_map/td,dcf->tcf/dot_general | solution.py:175
  84.7 2.7 fusion.107
  87.4 1.4 copy.193
  88.8 2.3 copy.195
  91.1 41.8 %all-gather.6.cloned.1.call-done = bf16[2,1024,384]{2,1,0:T(8,128)(2,1)} async-done(((bf16[2,32,384]{2,1,0:T(8,128)(2,1)}), bf16[2,1024,384]{2,1,0:T(8,128)(2,1)}) %all-gather.6.cloned.1.call-update) | async-done | bytes 1572880 | tf_op jit(solution)/shard_map/all_gather | solution.py:160
  132.9 2.7 fusion.108
  135.6 2.3 copy.192
  137.9 1.4 fusion.117
  139.3 1.2 fusion.115
  140.4 2.3 copy.194
  142.7 1.5 fusion.16
  144.2 1.8 fusion.30
  146.6 1.2 fusion.4
  148.0 21.3 %reduce-scatter.3.cloned.1.call-done = bf16[768,32]{0,1:T(8,128)(2,1)} async-done(((bf16[3072,32]{0,1:T(8,128)(2,1)}), bf16[768,32]{0,1:T(8,128)(2,1)}) %reduce-scatter.3.cloned.1.call-update) | async-done | bytes 49168 | tf_op jit(solution)/shard_map/reduce_scatter | solution.py:187
  169.3 0.9 fusion.47
  170.2 3.5 %collective-permute-start = (bf16[32,768]{1,0:T(8,128)(2,1)S(1)}, bf16[32,768]{1,0:T(8,128)(2,1)S(1)}, u32[]{:S(2)}, u32[]{:S(2)}) collective-permute-start(bf16[32,768]{1,0:T(8,128)(2,1)S(1)} %fusion.47), channel_id=1, source_target_pairs={{0,128},{1,129},{2,130},{3,131},{4,132},{5,133},{6,134},{7,135},{8... | collective-permute-start | bytes 147464 | tf_op jit(solution)/shard_map/ppermute | solution.py:26
  173.7 1.7 collective-permute-done
  175.4 8.9 %all_to_all.10 = bf16[4,32,768]{2,1,0:T(8,128)(2,1)S(1)} all-to-all(bf16[4,32,768]{2,1,0:T(8,128)(2,1)S(1)} %stack.38), channel_id=1, replica_groups=mesh['section'=2,'seq'=32,'tp'=4] {'tp'}, dimensions={0} | all-to-all | bytes 393216 | tf_op jit(solution)/shard_map/all_to_all | solution.py:16
  185.2 4.3 %fusion = f32[32,3,384]{2,0,1:T(8,128)S(1)} fusion(bf16[32,3072,1]{1,0,2:T(8,128)(2,1)S(1)} %reshape.1120, bf16[1,3072,3,384]{3,1,2,0:T(8,128)(2,1)} %param.10), kind=kOutput, calls=%fused_computation | convolution fusion | flops 226492416 | bytes 7421952 | tf_op jit(solution)/shard_map/td,dcf->tcf/dot_general | solution.py:175
  191.0 0.7 mul.505
  191.7 0.9 reshape_squeeze.53
  192.6 0.7 reduce_sum.159
  193.3 1.3 broadcast_multiply_fusion.1
  194.6 1.4 copy.198
  196.0 1.4 multiply_reduce_fusion.2
  197.5 1.4 copy.200
  198.8 0.7 add_rsqrt_fusion.1
  200.2 0.7 mul.491.clone
  200.9 1.6 mul.495
  202.5 1.5 sub.167.clone
  204.0 1.6 sub.169
  205.6 1.5 sub.171
  207.0 1.6 sub.175
  208.6 1.5 fusion.75
  210.1 0.7 slice_bitcast_fusion
  211.5 0.7 mul.501
  212.2 1.0 sub.172
  213.8 1.0 fusion.69
  216.3 1.4 copy.201
  217.7 0.8 fusion.112
  218.5 1.0 fusion.111
  219.6 0.7 pad_maximum_fusion.2
  220.3 0.9 concatenate.137
  221.2 1.5 fusion.53
  222.7 45.0 %all-gather.8.cloned.1.call-done = bf16[2,1024,384]{2,1,0:T(8,128)(2,1)} async-done(((bf16[2,32,384]{2,1,0:T(8,128)(2,1)}), bf16[2,1024,384]{2,1,0:T(8,128)(2,1)}) %all-gather.8.cloned.1.call-update) | async-done | bytes 1572880 | tf_op jit(solution)/shard_map/all_gather | solution.py:160
  267.7 2.7 fusion.106
  270.4 2.3 copy.208
  272.7 1.4 fusion.118
  274.1 1.1 fusion.116
  275.3 2.4 copy.209
  277.6 1.5 fusion.17
  279.1 1.5 fusion.31
  281.3 1.2 fusion.5
  283.2 20.8 %reduce-scatter.5.cloned.1.call-done = bf16[768,32]{0,1:T(8,128)(2,1)} async-done(((bf16[3072,32]{0,1:T(8,128)(2,1)}), bf16[768,32]{0,1:T(8,128)(2,1)}) %reduce-scatter.5.cloned.1.call-update) | async-done | bytes 49168 | tf_op jit(solution)/shard_map/reduce_scatter | solution.py:187
  304.1 1.5 fusion.59
  (203 shorter events, 14.8 us)
Async XLA Ops:
  7.2 139.4 %copy-start = (bf16[1,384,3072]{2,1,0:T(8,128)(2,1)S(1)}, bf16[1,384,3072]{2,1,0:T(8,128)(2,1)}, u32[]{:S(2)}) copy-start(bf16[1,384,3072]{2,1,0:T(8,128)(2,1)} %param.12) | copy-start | bytes 7077892
  8.8 65.9 %all-to-all-start = ((bf16[4,32,768]{2,1,0:T(8,128)(2,1)}), bf16[4,32,768]{2,1,0:T(8,128)(2,1)S(1)}, u32[]{:S(2)}, u32[]{:S(2)}) async-start(bf16[4,32,768]{2,1,0:T(8,128)(2,1)} %stack.36), calls=%async_computation | async-start | bytes 393216 | tf_op jit(solution)/shard_map/all_to_all | solution.py:16
  13.3 71.4 %all-gather.10.cloned.1.call-start = ((), (), s32[]{:S(2)}) async-start(), calls=%async_computation.8 | async-start | bytes 1622016 | tf_op jit(solution)/shard_map/all_gather | solution.py:161
  14.0 118.9 %all-gather.6.cloned.1.call-start = ((), (), s32[]{:S(2)}) async-start(), calls=%async_computation.4 | async-start | bytes 1622016 | tf_op jit(solution)/shard_map/all_gather | solution.py:160
  73.1 11.4 %copy-start.33 = (f32[64]{0:T(128)}, f32[64]{0:T(128)S(1)}, u32[]{:S(2)}) copy-start(f32[64]{0:T(128)S(1)} %get-tuple-element.47) | copy-start | bytes 772
  74.0 8.5 %copy-start.35 = (pred[384]{0:T(512)(128)(4,1)}, pred[384]{0:T(512)(128)(4,1)S(1)}, u32[]{:S(2)}) copy-start(pred[384]{0:T(512)(128)(4,1)S(1)} %fusion.93) | copy-start | bytes 1156
  74.2 7.6 %copy-start.32 = (f32[384]{0:T(512)}, f32[384]{0:T(512)S(1)}, u32[]{:S(2)}) copy-start(f32[384]{0:T(512)S(1)} %mul.464) | copy-start | bytes 4612
  74.3 8.3 %copy-start.25 = (f32[384]{0:T(512)}, f32[384]{0:T(512)S(1)}, u32[]{:S(2)}) copy-start(f32[384]{0:T(512)S(1)} %mul.474) | copy-start | bytes 4612
  74.3 10.2 %copy-start.10 = (f32[32,64]{1,0:T(8,128)}, f32[32,64]{1,0:T(8,128)S(1)}, u32[]{:S(2)}) copy-start(f32[32,64]{1,0:T(8,128)S(1)} %copy.182) | copy-start | bytes 24580
  74.4 10.1 %copy-start.11 = (f32[32,64]{1,0:T(8,128)}, f32[32,64]{1,0:T(8,128)S(1)}, u32[]{:S(2)}) copy-start(f32[32,64]{1,0:T(8,128)S(1)} %copy.187) | copy-start | bytes 24580
  74.6 8.0 %copy-start.8 = (f32[1,32,384]{2,1,0:T(8,128)}, f32[1,32,384]{2,1,0:T(8,128)S(1)}, u32[]{:S(2)}) copy-start(f32[1,32,384]{2,1,0:T(8,128)S(1)} %tile.20) | copy-start | bytes 147460
  74.6 7.9 %copy-start.9 = (f32[1,32,384]{2,1,0:T(8,128)}, f32[1,32,384]{2,1,0:T(8,128)S(1)}, u32[]{:S(2)}) copy-start(f32[1,32,384]{2,1,0:T(8,128)S(1)} %tile.21) | copy-start | bytes 147460
  74.7 110.0 %copy-start.30 = (pred[32]{0:T(512)(128)(4,1)}, pred[32]{0:T(512)(128)(4,1)S(1)}, u32[]{:S(2)}) copy-start(pred[32]{0:T(512)(128)(4,1)S(1)} %fusion.101) | copy-start | bytes 100
  79.8 3.6 %copy-start.36 = (s32[4]{0:T(128)S(1)}, s32[4]{0:T(128)}, u32[]{:S(2)}) copy-start(s32[4]{0:T(128)} %param.15) | copy-start | bytes 52
  82.7 1.7 copy-start.12
  83.3 86.0 %reduce-scatter.3.cloned.1.call-start = ((), (), s32[]{:S(2)}) async-start(), calls=%async_computation.5 | async-start | bytes 245760 | tf_op jit(solution)/shard_map/reduce_scatter | solution.py:187
  83.6 5.2 %copy-start.34 = (pred[6,64]{1,0:T(8,128)(4,1)}, pred[6,64]{1,0:T(8,128)(4,1)S(1)}, u32[]{:S(2)}) copy-start(pred[6,64]{1,0:T(8,128)(4,1)S(1)} %fusion.88) | copy-start | bytes 1156
  83.9 62.1 %copy-start.3 = (pred[32,1024]{1,0:T(8,128)(4,1)}, pred[32,1024]{1,0:T(8,128)(4,1)S(1)}, u32[]{:S(2)}) copy-start(pred[32,1024]{1,0:T(8,128)(4,1)S(1)} %broadcast_compare_fusion) | copy-start | bytes 98308
  142.7 3.3 %copy-start.2 = (f32[6,32,1024]{2,1,0:T(8,128)S(1)}, f32[6,32,1024]{2,1,0:T(8,128)}, u32[]{:S(2)}) copy-start(f32[6,32,1024]{2,1,0:T(8,128)} %get-tuple-element.52) | copy-start | bytes 2359300
  142.7 3.3 %copy-start.5 = (bf16[1,1,1024,384]{2,3,1,0:T(8,128)(2,1)S(1)}, bf16[1,1,1024,384]{2,3,1,0:T(8,128)(2,1)}, u32[]{:S(2)}) copy-start(bf16[1,1,1024,384]{2,3,1,0:T(8,128)(2,1)} %copy.195) | copy-start | bytes 2359300
  146.0 23.3 %copy-start.18 = (bf16[32,768]{1,0:T(8,128)(2,1)S(1)}, bf16[32,768]{1,0:T(8,128)(2,1)}, u32[]{:S(2)}) copy-start(bf16[32,768]{1,0:T(8,128)(2,1)} %param.9) | copy-start | bytes 147460
  147.8 119.9 %all-gather.8.cloned.1.call-start = ((), (), s32[]{:S(2)}) async-start(), calls=%async_computation.6 | async-start | bytes 1622016 | tf_op jit(solution)/shard_map/all_gather | solution.py:160
  148.0 36.7 %copy-start.26 = (f32[768]{0:T(1024)}, f32[768]{0:T(1024)S(1)}, u32[]{:S(2)}) copy-start(f32[768]{0:T(1024)S(1)} %get-tuple-element.2) | copy-start | bytes 9220
  148.0 36.7 %copy-start.28 = (f32[768]{0:T(1024)}, f32[768]{0:T(1024)S(1)}, u32[]{:S(2)}) copy-start(f32[768]{0:T(1024)S(1)} %get-tuple-element.3) | copy-start | bytes 9220
  170.2 3.5 %copy-start.16 = (bf16[32,768]{1,0:T(8,128)(2,1)}, bf16[32,768]{1,0:T(8,128)(2,1)S(1)}, u32[]{:S(2)}) copy-start(bf16[32,768]{1,0:T(8,128)(2,1)S(1)} %fusion.47) | copy-start | bytes 147460
  170.2 5.2 %collective-permute-start = (bf16[32,768]{1,0:T(8,128)(2,1)S(1)}, bf16[32,768]{1,0:T(8,128)(2,1)S(1)}, u32[]{:S(2)}, u32[]{:S(2)}) collective-permute-start(bf16[32,768]{1,0:T(8,128)(2,1)S(1)} %fusion.47), channel_id=1, source_target_pairs={{0,128},{1,129},{2,130},{3,131},{4,132},{5,133},{6,134},{7,135},{8... | collective-permute-start | bytes 147464 | tf_op jit(solution)/shard_map/ppermute | solution.py:26
  175.4 9.3 %copy-start.19 = (bf16[32,768]{1,0:T(8,128)(2,1)}, bf16[32,768]{1,0:T(8,128)(2,1)S(1)}, u32[]{:S(2)}) copy-start(bf16[32,768]{1,0:T(8,128)(2,1)S(1)} %collective-permute-done) | copy-start | bytes 147460
  190.3 0.6 copy-start.21
  199.6 0.6 copy-start.22
  214.8 0.6 copy-start.14
  216.1 88.0 %reduce-scatter.5.cloned.1.call-start = ((), (), s32[]{:S(2)}) async-start(), calls=%async_computation.7 | async-start | bytes 245760 | tf_op jit(solution)/shard_map/reduce_scatter | solution.py:187
  222.7 50.0 %copy-start.7 = (bf16[32,6,64]{2,0,1:T(8,128)(2,1)S(1)}, bf16[32,6,64]{2,0,1:T(8,128)(2,1)}, u32[]{:S(2)}) copy-start(bf16[32,6,64]{2,0,1:T(8,128)(2,1)} %fusion.53) | copy-start | bytes 73732
  270.4 3.7 %copy-start.4 = (pred[32,1024]{1,0:T(8,128)(4,1)S(1)}, pred[32,1024]{1,0:T(8,128)(4,1)}, u32[]{:S(2)}) copy-start(pred[32,1024]{1,0:T(8,128)(4,1)} %copy-done.3) | copy-start | bytes 98308
  275.3 3.8 %copy-start.1 = (f32[6,32,1024]{2,1,0:T(8,128)S(1)}, f32[6,32,1024]{2,1,0:T(8,128)}, u32[]{:S(2)}) copy-start(f32[6,32,1024]{2,1,0:T(8,128)} %get-tuple-element.54) | copy-start | bytes 2359300
  277.6 3.0 copy-start.6
  280.7 1.9 copy-start.13
  280.7 1.9 copy-start.15
  280.7 1.9 copy-start.23
  280.7 1.9 copy-start.24
  280.7 23.3 %copy-start.17 = (bf16[32,768]{1,0:T(8,128)(2,1)S(1)}, bf16[32,768]{1,0:T(8,128)(2,1)}, u32[]{:S(2)}) copy-start(bf16[32,768]{1,0:T(8,128)(2,1)} %copy-done.16) | copy-start | bytes 147460
  280.7 23.3 %copy-start.20 = (bf16[32,768]{1,0:T(8,128)(2,1)S(1)}, bf16[32,768]{1,0:T(8,128)(2,1)}, u32[]{:S(2)}) copy-start(bf16[32,768]{1,0:T(8,128)(2,1)} %copy-done.19) | copy-start | bytes 147460
  280.7 23.3 %copy-start.27 = (f32[768]{0:T(1024)S(1)}, f32[768]{0:T(1024)}, u32[]{:S(2)}) copy-start(f32[768]{0:T(1024)} %copy-done.26) | copy-start | bytes 9220
  280.7 23.3 %copy-start.29 = (f32[768]{0:T(1024)S(1)}, f32[768]{0:T(1024)}, u32[]{:S(2)}) copy-start(f32[768]{0:T(1024)} %copy-done.28) | copy-start | bytes 9220
  280.8 23.3 %copy-start.31 = (pred[32]{0:T(512)(128)(4,1)S(1)}, pred[32]{0:T(512)(128)(4,1)}, u32[]{:S(2)}) copy-start(pred[32]{0:T(512)(128)(4,1)} %copy-done.30) | copy-start | bytes 100
Sparse Core Ops, SparseCore 0:
  16.7 55.4 all-gather.9
  83.4 49.4 all-gather.5
  148.0 21.2 reduce-scatter.2
  216.2 51.4 all-gather.7
  282.7 21.3 reduce-scatter.4
